TPU v7x, 256 devices: a whole 4x4x8 slice. The times are simulated.
256 devices in a mesh: dp: 4 (over x), tensor: 64 (over y, z, core).
Axes of the slice: x: 4, y: 4, z: 8, core: 2. Of those that a mesh axis runs over, the one named last changes fastest.
Arguments:
- grad_out: bfloat16 [4096, 8192], P('dp', 'tensor'), may hold values from -6 to 6
- acts: bfloat16 [4096, 16384], P('dp', 'tensor'), may hold values from -6 to 6
- weight: bfloat16 [8192, 16384], P('tensor'), may hold values from -0.078125 to 0.078125
- block_mask: int32 [64, 128], replicated, may hold values from 0 to 1, as said below
Outputs:
- grad_acts: bfloat16 [4096, 16384], P('dp', 'tensor')
- grad_weight: float32 [8192, 16384], P(('dp', 'tensor'))
Inputs may be any that keep to these rules, and one draw needn't show every extreme that they name: `block_mask`: kept shares differ between groups of 2 consecutive block columns, from about three twentieths to nine twentieths.
All inputs are finite; a program needn't handle non-finite values.
Results may differ from a plain program's by a relative error of at most 0.001.
Values may be sent and summed in bfloat16 or wider, within the bound.
A program may use at most 128 MiB of HBM per device.

v0:
```python
import jax
import jax.numpy as jnp
from jax import lax
from jax.sharding import PartitionSpec as P


def expand_mask(mask, side):
    rows, cols = mask.shape
    full = jnp.broadcast_to(mask[:, None, :, None], (rows, side, cols, side))
    return full.reshape(rows * side, cols * side)


def body(grad_out, acts, weight, block_mask):
    tensor_count = lax.axis_size("tensor")
    group_count = lax.axis_size("dp")
    position = lax.axis_index("tensor")
    d_tile = weight.shape[0]
    full_width = weight.shape[1]
    ff_tile = acts.shape[1]
    side = full_width // block_mask.shape[1]
    total_rows = d_tile * tensor_count
    row_mask = lax.dynamic_slice_in_dim(block_mask, position * (d_tile // side), d_tile // side, 0)
    kept = weight * expand_mask(row_mask, side).astype(jnp.bfloat16)
    columns = lax.all_to_all(kept, "tensor", split_axis=1, concat_axis=0, tiled=True)
    piece = lax.all_gather(grad_out, "tensor", axis=1, tiled=True)
    input_grad = jnp.dot(piece, columns, preferred_element_type=jnp.float32)
    grad_rows = lax.dot_general(
        piece, acts, (((0,), (0,)), ((), ())), preferred_element_type=jnp.float32
    )
    weight_grad = grad_rows
    input_grad, weight_grad = (input_grad, weight_grad)
    grad_acts = input_grad.astype(jnp.bfloat16)
    col_mask = lax.dynamic_slice_in_dim(
        block_mask, position * (ff_tile // side), ff_tile // side, 1
    )
    scale_factor = 1.0 / (grad_out.shape[0] * group_count) ** 0.5
    weight_grad = weight_grad * expand_mask(col_mask, side).astype(jnp.float32) * scale_factor
    quarter = total_rows // (group_count * tensor_count)
    reordered = weight_grad.reshape(group_count, tensor_count, quarter, ff_tile)
    reordered = jnp.transpose(reordered, (1, 0, 2, 3)).reshape(total_rows, ff_tile)
    owned = lax.all_to_all(reordered, "tensor", split_axis=0, concat_axis=1, tiled=True)
    grad_weight = lax.psum_scatter(owned, "dp", scatter_dimension=0, tiled=True)
    return (grad_acts, grad_weight)


def solution(mesh):
    in_specs = (P("dp", "tensor"), P("dp", "tensor"), P("tensor", None), P())
    out_specs = (P("dp", "tensor"), P(("dp", "tensor"), None))
    return jax.shard_map(body, mesh=mesh, in_specs=in_specs, out_specs=out_specs, check_vma=False)
```

profile of v0, /device:TPU:1, one launch (start us, length us, event | category | flops | bytes accessed | tf_op | source)
XLA Modules:
  0.0 497.6 jit_solution(10132291511642374837)
XLA Ops:
  7.2 0.0 copy-start
  7.2 0.0 all-gather.2.cloned.1.call-start
  7.2 0.7 all-gather.2.cloned.1.call-update
  7.9 0.0 reduce-scatter.4.cloned.1.call-start
  8.0 0.8 dynamic-slice_convert_fusion
  8.8 113.1 %all-gather.2.cloned.1.call-done = bf16[1024,8192]{1,0:T(8,128)(2,1)} async-done(((bf16[1024,128]{1,0:T(8,128)(2,1)}), bf16[1024,8192]{1,0:T(8,128)(2,1)}) %all-gather.2.cloned.1.call-update) | async-done | bytes 16777232 | tf_op jit(solution)/shard_map/all_gather | solution.py:25
  121.9 5.5 %broadcast_in_dim.16 = f32[64,128,2,128]{3,2,1,0:T(2,128)} broadcast(f32[64,2]{1,0:T(8,128)S(1)} %dynamic-slice_convert_fusion), dimensions={0,2} | broadcast | bytes 8389120 | tf_op jit(solution)/shard_map/broadcast_in_dim | solution.py:9
  127.4 0.0 copy-done
  127.4 13.7 %fusion = f32[8192,256]{1,0:T(8,128)S(1)} fusion(bf16[1024,8192]{1,0:T(8,128)(2,1)} %all-gather.2.cloned.1.call-done, bf16[1024,256]{1,0:T(8,128)(2,1)S(1)} %copy-done, f32[1024,8,2,128]{3,2,1,0:T(2,128)} %bitcast.29), kind=kOutput, calls=%fused_computation.1 | convolution fusion | flops 4299161600 | bytes 34078720 | tf_op jit(solution)/shard_map/dot_general | solution.py:27
  141.1 1.7 copy.17
  142.7 192.2 %all_to_all.38 = f32[64,128,256]{2,1,0:T(8,128)} all-to-all(f32[64,128,256]{2,1,0:T(8,128)S(1)} %bitcast.24), channel_id=1, replica_groups=mesh['dp'=4,'tensor'=64] {'tensor'}, dimensions={0} | all-to-all | bytes 16777216 | tf_op jit(solution)/shard_map/all_to_all | solution.py:41
  334.9 9.0 %copy.18 = f32[128,64,256]{0,2,1:T(8,128)} copy(f32[128,64,256]{2,0,1:T(8,128)} %bitcast.25) | data formatting | bytes 16777216 | tf_op jit(solution)/shard_map/all_to_all | solution.py:41
  343.9 9.0 %copy.21 = f32[128,16384]{1,0:T(8,128)} copy(f32[128,16384]{0,1:T(8,128)} %bitcast.26) | data formatting | bytes 16777216
  352.8 0.0 reduce-scatter.4.cloned.1.call-update
  352.9 6.4 %copy.15 = bf16[128,16384]{0,1:T(8,128)(2,1)} copy(bf16[128,16384]{1,0:T(8,128)(2,1)} %param.6) | data formatting | bytes 8388608 | tf_op args[2]
  359.2 0.7 convert_bitcast_fusion
  359.9 0.1 broadcast_bitcast_fusion
  360.0 10.0 %broadcast_multiply_fusion = bf16[128,16384]{0,1:T(8,128)(2,1)S(1)} fusion(bf16[128,16384]{0,1:T(8,128)(2,1)} %copy.15, bf16[16384]{0:T(1024)(128)(2,1)S(1)} %broadcast_bitcast_fusion), kind=kLoop, calls=%fused_computation.2 | loop fusion | flops 2097152 | bytes 8421376 | tf_op jit(solution)/shard_map/mul | solution.py:23
  370.0 101.7 %all_to_all.39 = bf16[128,64,256]{0,2,1:T(8,128)(2,1)} all-to-all(bf16[128,64,256]{0,2,1:T(8,128)(2,1)S(1)} %bitcast.27), channel_id=1, replica_groups=mesh['dp'=4,'tensor'=64] {'tensor'}, dimensions={1} | all-to-all | bytes 8388608 | tf_op jit(solution)/shard_map/all_to_all | solution.py:24
  471.7 6.4 %copy.16 = bf16[64,128,256]{2,1,0:T(8,128)(2,1)} copy(bf16[64,128,256]{1,2,0:T(8,128)(2,1)} %bitcast.28) | data formatting | bytes 8388608 | tf_op jit(solution)/shard_map/all_to_all | solution.py:24
  478.1 0.0 copy-start.1
  478.1 11.6 %fusion.1 = bf16[1024,256]{0,1:T(8,128)(2,1)S(1)} fusion(bf16[8192,256]{1,0:T(8,128)(2,1)} %bitcast.31, bf16[1024,8192]{1,0:T(8,128)(2,1)} %all-gather.2.cloned.1.call-done), kind=kOutput, calls=%fused_computation.4 | convolution fusion | flops 4295229440 | bytes 21495808 | tf_op jit(solution)/shard_map/dot_general | solution.py:26
  489.8 1.0 copy.19
  490.8 0.0 reduce-scatter.4.cloned.1.call-done
  490.8 0.0 copy-done.1
Async XLA Ops:
  7.2 120.2 %copy-start = (bf16[1024,256]{1,0:T(8,128)(2,1)S(1)}, bf16[1024,256]{1,0:T(8,128)(2,1)}, u32[]{:S(2)}) copy-start(bf16[1024,256]{1,0:T(8,128)(2,1)} %param.5) | copy-start | bytes 1572868
  7.2 114.8 %all-gather.2.cloned.1.call-start = ((), (), s32[]{:S(2)}) async-start(), calls=%async_computation.3 | async-start | bytes 17039360 | tf_op jit(solution)/shard_map/all_gather | solution.py:25
  7.9 482.8 %reduce-scatter.4.cloned.1.call-start = ((), (), s32[]{:S(2)}) async-start(), calls=%async_computation.4 | async-start | bytes 10485760
  478.1 12.7 %copy-start.1 = (bf16[1024,256]{1,0:T(8,128)(2,1)S(1)}, bf16[1024,256]{1,0:T(8,128)(2,1)}, u32[]{:S(2)}) copy-start(bf16[1024,256]{1,0:T(8,128)(2,1)} %param.5) | copy-start | bytes 1572868
Sparse Core Ops, SparseCore 0:
  10.6 111.3 all-gather.1
  353.0 79.4 reduce-scatter.3
where the time goes:
time: 498 us
  blocking collectives  294 us (59%)
  waiting for transfers between devices  114 us (23%)
  local copies, waits for them, and re-layouts  38.9 us (8%)
  matrix products  25.3 us (5%)
  between operations  14.1 us (3%)
  other arithmetic  11.6 us (2%)
    all_to_all x1, blocking collectives, body(): lax.all_to_all(reordered, 'tensor', split_axis=0, concat_axis=1, tiled=True)  192 us
    all_gather x1, waiting for transfers between devices, body(): piece = lax.all_gather(grad_out, 'tensor', axis=1, tiled=True)  113 us
    all_to_all x1, blocking collectives, body(): lax.all_to_all(kept, 'tensor', split_axis=1, concat_axis=0, tiled=True)  102 us
    unnamed x7, local copies, waits for them, and re-layouts  16.3 us
    dot_general x1, matrix products, body(): lax.dot_general(piece, acts, (((0,), (0,)), ((), ())), preferred_element_...  13.7 us
    dot_general x1, matrix products, body(): input_grad = jnp.dot(piece, columns, preferred_element_type=jnp.float32)  11.6 us
    mul x1, other arithmetic, body(): kept = weight * expand_mask(row_mask, side).astype(jnp.bfloat16)  10 us
  transfers between devices with their start and end apart: 2, of which 1 were waited for; matrix products, arithmetic and copies ran while one was open for 7% of the time, Pallas kernels for 0%

commit v1 on v0

--- a/solution.py
+++ b/solution.py
@@ -22,7 +22,9 @@
     row_mask = lax.dynamic_slice_in_dim(block_mask, position * (d_tile // side), d_tile // side, 0)
     kept = weight * expand_mask(row_mask, side).astype(jnp.bfloat16)
     columns = lax.all_to_all(kept, "tensor", split_axis=1, concat_axis=0, tiled=True)
-    piece = lax.all_gather(grad_out, "tensor", axis=1, tiled=True)
+    piece = jnp.concatenate(
+        lax.all_to_all(jnp.stack([grad_out] * lax.axis_size("tensor")), "tensor", 0, 0), axis=1
+    )
     input_grad = jnp.dot(piece, columns, preferred_element_type=jnp.float32)
     grad_rows = lax.dot_general(
         piece, acts, (((0,), (0,)), ((), ())), preferred_element_type=jnp.float32

time: 498 us -> 780 us (1.57)
  waiting for transfers between devices: 114 us -> 365 us
  local copies, waits for them, and re-layouts: 38.9 us -> 61.8 us
  starting transfers between devices: 0.08 us -> 13.5 us
    all_to_all x0 -> x1, waiting for transfers between devices: none -> 365 us  [body(): lax.all_to_all(jnp.stack([grad_out] * lax.axis_size('tensor')), 'tensor',...]
    all_gather x1 -> x0, waiting for transfers between devices: 113 us -> none  [body(): piece = lax.all_gather(grad_out, 'tensor', axis=1, tiled=True)]
    reshape x0 -> x1, local copies, waits for them, and re-layouts: none -> 22.4 us  [body(): jnp.concatenate(lax.all_to_all(jnp.stack([grad_out] * lax.axis_size('tens...]
    all_to_all x0 -> x1, starting transfers between devices: none -> 13.5 us  [body(): lax.all_to_all(jnp.stack([grad_out] * lax.axis_size('tensor')), 'tensor',...]
    unnamed x7 -> x8, local copies, waits for them, and re-layouts: 16.3 us -> 9.98 us
  transfers between devices with their start and end apart: 2 -> 2, of which waited for: 1 -> 1; matrix products, arithmetic and copies ran while one was open for 7% -> 3% of each run, Pallas kernels for 0% -> 0%
where the time goes in v1:
time: 780 us; the launch traced here: 779 us
  waiting for transfers between devices  365 us (47%)
  blocking collectives  294 us (38%)
  local copies, waits for them, and re-layouts  61.8 us (8%)
  matrix products  24.7 us (3%)
  between operations  14.1 us (2%)
  starting transfers between devices  13.5 us (2%)
    all_to_all x1, waiting for transfers between devices, body(): lax.all_to_all(jnp.stack([grad_out] * lax.axis_size('tensor')), 'tensor',...  365 us
    all_to_all x1, blocking collectives, body(): lax.all_to_all(reordered, 'tensor', split_axis=0, concat_axis=1, tiled=True)  192 us
    all_to_all x1, blocking collectives, body(): lax.all_to_all(kept, 'tensor', split_axis=1, concat_axis=0, tiled=True)  102 us
    reshape x1, local copies, waits for them, and re-layouts, body(): jnp.concatenate(lax.all_to_all(jnp.stack([grad_out] * lax.axis_size('tens...  22.4 us
  transfers between devices with their start and end apart: 2, of which 1 were waited for; matrix products, arithmetic and copies ran while one was open for 3% of the time, Pallas kernels for 0%

profile of v1, /device:TPU:1, one launch (start us, length us, event | category | flops | bytes accessed | tf_op | source)
XLA Modules:
  0.0 778.7 jit_solution(13017810349199021666)
XLA Ops:
  7.2 0.0 copy-start
  7.2 7.0 stack.2
  14.2 0.0 copy-start.2
  14.2 13.5 %all-to-all-start.1 = ((bf16[64,1024,128]{2,1,0:T(8,128)(2,1)}), bf16[64,1024,128]{2,1,0:T(8,128)(2,1)}, u32[]{:S(2)}, u32[]{:S(2)}) async-start(bf16[64,1024,128]{2,1,0:T(8,128)(2,1)} %stack.2), calls=%async_computation.1 | async-start | bytes 33554432 | tf_op jit(solution)/shard_map/all_to_all | solution.py:26
  27.7 0.0 reduce-scatter.4.cloned.1.call-start
  27.7 0.0 copy-done.2
  27.7 0.1 dynamic-slice_convert_fusion
  27.8 365.4 %all-to-all-done.1 = bf16[64,1024,128]{2,1,0:T(8,128)(2,1)} async-done(((bf16[64,1024,128]{2,1,0:T(8,128)(2,1)}), bf16[64,1024,128]{2,1,0:T(8,128)(2,1)}, u32[]{:S(2)}, u32[]{:S(2)}) %all-to-all-start.1) | async-done | bytes 16777248 | tf_op jit(solution)/shard_map/all_to_all | solution.py:26
  393.2 22.4 %copy.19 = bf16[1024,64,128]{0,2,1:T(8,128)(2,1)} copy(bf16[1024,64,128]{2,0,1:T(8,128)(2,1)} %bitcast.4) | data formatting | bytes 33554432 | tf_op jit(solution)/shard_map/reshape | solution.py:25
  415.6 5.4 broadcast_in_dim.16
  421.0 0.0 copy-done
  421.0 13.1 %fusion = f32[8192,256]{1,0:T(8,128)S(1)} fusion(bf16[1024,8192]{0,1:T(8,128)(2,1)} %bitcast.39, bf16[1024,256]{1,0:T(8,128)(2,1)S(1)} %copy-done, f32[1024,8,2,128]{3,2,1,0:T(2,128)} %bitcast.40), kind=kOutput, calls=%fused_computation.1 | convolution fusion | flops 4299161600 | bytes 34078720 | tf_op jit(solution)/shard_map/dot_general | solution.py:29
  434.1 1.7 copy.20
  435.8 192.1 %all_to_all.40 = f32[64,128,256]{2,1,0:T(8,128)} all-to-all(f32[64,128,256]{2,1,0:T(8,128)S(1)} %bitcast.42), channel_id=1, replica_groups=mesh['dp'=4,'tensor'=64] {'tensor'}, dimensions={0} | all-to-all | bytes 16777216 | tf_op jit(solution)/shard_map/all_to_all | solution.py:43
  627.8 9.0 %copy.21 = f32[128,64,256]{0,2,1:T(8,128)} copy(f32[128,64,256]{2,0,1:T(8,128)} %bitcast.43) | data formatting | bytes 16777216 | tf_op jit(solution)/shard_map/all_to_all | solution.py:43
  636.8 9.0 %copy.24 = f32[128,16384]{1,0:T(8,128)} copy(f32[128,16384]{0,1:T(8,128)} %bitcast.44) | data formatting | bytes 16777216
  645.8 0.0 reduce-scatter.4.cloned.1.call-update
  645.8 0.1 broadcast_bitcast_fusion
  645.9 4.7 broadcast_multiply_fusion
  650.6 6.4 copy.18
  657.0 0.0 copy-start.1
  657.0 102.4 %all_to_all.41 = bf16[128,64,256]{0,2,1:T(8,128)(2,1)} all-to-all(bf16[128,64,256]{0,2,1:T(8,128)(2,1)} %bitcast.45), channel_id=1, replica_groups=mesh['dp'=4,'tensor'=64] {'tensor'}, dimensions={1} | all-to-all | bytes 8388608 | tf_op jit(solution)/shard_map/all_to_all | solution.py:24
  759.3 11.6 %fusion.9 = bf16[1024,256]{0,1:T(8,128)(2,1)S(1)} fusion(bf16[128,64,256]{0,2,1:T(8,128)(2,1)} %all_to_all.41, bf16[64,1024,128]{2,1,0:T(8,128)(2,1)} %all-to-all-done.1), kind=kOutput, calls=%fused_computation.7 | convolution fusion | flops 4295229440 | bytes 21495808 | tf_op jit(solution)/shard_map/dot_general | solution.py:28
  770.9 1.0 copy.22
  771.9 0.0 reduce-scatter.4.cloned.1.call-done
  771.9 0.0 copy-done.1
  (1 shorter events, 0.0 us)
Async XLA Ops:
  7.2 413.8 %copy-start = (bf16[1024,256]{1,0:T(8,128)(2,1)S(1)}, bf16[1024,256]{1,0:T(8,128)(2,1)}, u32[]{:S(2)}) copy-start(bf16[1024,256]{1,0:T(8,128)(2,1)} %param.5) | copy-start | bytes 1572868
  14.2 13.5 %copy-start.2 = (s32[64,128]{1,0:T(8,128)S(1)}, s32[64,128]{1,0:T(8,128)}, u32[]{:S(2)}) copy-start(s32[64,128]{1,0:T(8,128)} %param.7) | copy-start | bytes 98308
  14.2 379.0 %all-to-all-start.1 = ((bf16[64,1024,128]{2,1,0:T(8,128)(2,1)}), bf16[64,1024,128]{2,1,0:T(8,128)(2,1)}, u32[]{:S(2)}, u32[]{:S(2)}) async-start(bf16[64,1024,128]{2,1,0:T(8,128)(2,1)} %stack.2), calls=%async_computation.1 | async-start | bytes 33554432 | tf_op jit(solution)/shard_map/all_to_all | solution.py:26
  27.7 744.2 %reduce-scatter.4.cloned.1.call-start = ((), (), s32[]{:S(2)}) async-start(), calls=%async_computation.4 | async-start | bytes 10485760
  657.0 114.9 %copy-start.1 = (bf16[1024,256]{1,0:T(8,128)(2,1)S(1)}, bf16[1024,256]{1,0:T(8,128)(2,1)}, u32[]{:S(2)}) copy-start(bf16[1024,256]{1,0:T(8,128)(2,1)} %param.5) | copy-start | bytes 1572868
Sparse Core Ops, SparseCore 0:
  645.9 79.5 reduce-scatter.3
